TPU v7x, 32 devices: a whole 2x2x4 slice. The times are simulated.
32 devices in a mesh: clip: 4 (over z), frame: 4 (over x, core), row: 2 (over y).
Axes of the slice: x: 2, y: 2, z: 4, core: 2. Of those that a mesh axis runs over, the one named last changes fastest.
Arguments:
- features: bfloat16 [4, 16, 2, 32, 384], P('clip', 'frame', 'row'), may hold values from -6 to 6
- time_weight: bfloat16 [3, 384, 768], replicated, may hold values from -0.1875 to 0.1875
- time_bias: float32 [768], replicated, may hold values from -3 to 3
- space_weight: bfloat16 [3, 3, 384, 192], replicated, may hold values from -0.109375 to 0.109375
- pixel_grads: bfloat16 [4, 32, 4, 64, 192], P('clip', ('frame', 'row')), may hold values from -6 to 6
- frame_order: int32 [4, 4, 8], P('clip', 'frame'), may hold values from 0 to 7, each once within a row
Outputs:
- input_grad: bfloat16 [4, 16, 2, 32, 384], P('clip', 'frame', 'row')
- weight_grad: float32 [663552], P(('frame', 'row'))
Inputs may be any that keep to these rules, and one draw needn't show every extreme that they name: `frame_order`: for each clip and frame group, the row lists every one of the group's 8 output frames exactly once.
All inputs are finite; a program needn't handle non-finite values.
Results may differ from a plain program's by a relative error of at most 0.0049.
Values may be sent and summed in bfloat16 or wider, within the bound.
No kernel may reach another device: no remote copies, remote signals or barrier semaphores. Data moves between devices by JAX's collectives and lax.ppermute only.
A program may use at most 64 MiB of HBM per device.

v0:
```python
import math
import jax
import jax.numpy as jnp
from jax import lax
from jax.sharding import PartitionSpec as P


def passed_along(block, axis, distance):
    devices = range(lax.axis_size(axis))
    route = [(i - distance, i) for i in devices if i - distance in devices]
    return lax.ppermute(block, axis, route)


def extended_2(x, sides, width):
    for axis, dim in sides:
        count, length = (lax.axis_size(axis), x.shape[dim])
        up = [(i, (i + 1) % count) for i in range(count - 1)]
        down = [(j, i) for i, j in up]
        last = lax.slice_in_dim(x, length - width, length, axis=dim)
        initial = lax.slice_in_dim(x, 0, width, axis=dim)
        before = lax.ppermute(last, axis, up)
        after = lax.ppermute(initial, axis, down)
        x = jnp.concatenate([before, x, after], axis=dim)
    return x


def time_conv(extended, time_weight, time_bias):
    frames = extended.shape[1] - 2
    total = time_bias
    for offset in range(3):
        total = total + jnp.einsum(
            "cfhwi,io->cfhwo",
            extended[:, offset : offset + frames],
            time_weight[offset],
            preferred_element_type=jnp.float32,
        )
    return total.astype(jnp.bfloat16)


def local(features, time_weight, time_bias, space_weight, pixel_grads, frame_order):
    frames = features.shape[1]
    rows = features.shape[2]
    width = features.shape[3]
    channels = features.shape[4]
    up_rows = 2 * rows
    up_width = 2 * width
    band_count = lax.axis_size("row")
    prior = passed_along(features[:, frames - 2 :], "frame", 1)
    extended = jnp.concatenate((prior, features), axis=1)
    bordered = extended_2(extended, (("row", 2),), 1)
    activation = time_conv(bordered, time_weight, time_bias)
    position = jnp.arange(rows + 2) + lax.axis_index("row") * rows - 1
    inside = (position >= 0) & (position < band_count * rows)
    activation = jnp.where(
        inside[None, None, :, None, None], activation, jnp.zeros((), jnp.bfloat16)
    )
    upsampled = jnp.stack((activation[..., :channels], activation[..., channels:]), axis=2)
    upsampled = upsampled.reshape(1, 2 * frames, rows + 2, width, channels)
    upsampled = jnp.repeat(jnp.repeat(upsampled, 2, axis=2), 2, axis=3)[:, :, 1 : up_rows + 3]
    padded_act = jnp.pad(upsampled, ((0, 0), (0, 0), (0, 0), (1, 1), (0, 0)))
    inverse = jnp.argsort(frame_order[0, 0])
    stored = lax.all_to_all(pixel_grads, "row", split_axis=2, concat_axis=1, tiled=True)
    ordered = jnp.take(stored, inverse, axis=1)
    grad_band = extended_2(ordered, (("row", 2),), 1)
    grad_center = grad_band[:, :, 1 : up_rows + 1]
    tap_terms = []
    for tap_row in range(3):
        for tap_col in range(3):
            window = padded_act[:, :, tap_row : tap_row + up_rows, tap_col : tap_col + up_width]
            tap_terms.append(
                jnp.einsum(
                    "cfhwi,cfhwo->io", window, grad_center, preferred_element_type=jnp.float32
                )
            )
    weight_terms = jnp.stack(tap_terms).reshape(-1)
    out_pixels = (
        2
        * frames
        * up_rows
        * up_width
        * lax.axis_size("clip")
        * lax.axis_size("frame")
        * band_count
    )
    shard = lax.psum_scatter(weight_terms, ("frame", "row"), scatter_dimension=0, tiled=True)
    summed = lax.psum(shard, "clip")
    weight_grad = summed * (1.0 / math.sqrt(out_pixels))
    padded_grad = jnp.pad(grad_band, ((0, 0), (0, 0), (0, 0), (1, 1), (0, 0)))
    up_grad = jnp.zeros((1, 2 * frames, up_rows, up_width, channels), jnp.float32)
    for tap_row in range(3):
        for tap_col in range(3):
            window = padded_grad[
                :, :, 2 - tap_row : 2 - tap_row + up_rows, 2 - tap_col : 2 - tap_col + up_width
            ]
            up_grad = up_grad + jnp.einsum(
                "cfhwo,io->cfhwi",
                window,
                space_weight[tap_row, tap_col],
                preferred_element_type=jnp.float32,
            )
    pooled = up_grad.reshape(1, frames, 2, rows, 2, width, 2, channels).sum(axis=(4, 6))
    act_grad = (
        pooled.transpose(0, 1, 3, 4, 2, 5)
        .reshape(1, frames, rows, width, 2 * channels)
        .astype(jnp.bfloat16)
    )
    later = passed_along(act_grad[:, :2], "frame", -1)
    tail = jnp.concatenate((act_grad, later), axis=1)
    input_grad = jnp.zeros((1, frames, rows, width, channels), jnp.float32)
    for offset in range(3):
        input_grad = input_grad + jnp.einsum(
            "cfhwo,io->cfhwi",
            tail[:, 2 - offset : 2 - offset + frames],
            time_weight[offset],
            preferred_element_type=jnp.float32,
        )
    return (input_grad.astype(jnp.bfloat16), weight_grad)


def solution(mesh):
    return jax.shard_map(
        local,
        mesh=mesh,
        in_specs=(
            P("clip", "frame", "row", None, None),
            P(),
            P(),
            P(),
            P("clip", ("frame", "row"), None, None, None),
            P("clip", "frame", None),
        ),
        out_specs=(P("clip", "frame", "row", None, None), P(("frame", "row"))),
        check_vma=False,
    )
```

profile of v0, /device:TPU:0, one launch (start us, length us, event | category | flops | bytes accessed | tf_op | source)
XLA Modules:
  0.0 169.0 jit_solution(18252574621571368024)
XLA Ops:
  7.2 1.9 %copy.29 = bf16[1,4,4,64,192]{4,3,1,0,2:T(8,128)(2,1)} copy(bf16[1,4,4,64,192]{4,3,2,1,0:T(8,128)(2,1)} %param.10) | data formatting | bytes 786432 | tf_op args[4]
  9.1 4.3 %all-to-all-start = ((bf16[1,4,4,64,192]{4,3,1,0,2:T(8,128)(2,1)}), bf16[1,4,4,64,192]{4,3,1,0,2:T(8,128)(2,1)S(1)}, u32[]{:S(2)}, u32[]{:S(2)}) async-start(bf16[1,4,4,64,192]{4,3,1,0,2:T(8,128)(2,1)} %copy.29), calls=%async_computation | async-start | bytes 1048576 | tf_op jit(solution)/shard_map/all_to_all | solution.py:62
  13.4 1.7 %collective-permute-start.3 = (bf16[1,2,1,32,384]{4,3,2,1,0:T(8,128)(2,1)S(1)}, bf16[1,2,1,32,384]{4,3,2,1,0:T(8,128)(2,1)S(1)}, u32[]{:S(2)}, u32[]{:S(2)}) collective-permute-start(bf16[1,2,1,32,384]{4,3,2,1,0:T(8,128)(2,1)S(1)} %slice.163), channel_id=1, source_target_pairs={{0,2},{2,4},{4,6},{1,3},{3,5},{5,7},{8,10},{10,12},{12,14},{9,11},... | collective-permute-start | bytes 147464 | tf_op jit(solution)/shard_map/ppermute | solution.py:11
  15.1 1.0 sort.17
  16.1 0.6 dynamic-slice
  17.4 1.3 collective-permute-start.5
  18.7 4.6 %collective-permute-start.4 = (bf16[1,6,1,32,384]{4,3,2,1,0:T(8,128)(2,1)S(1)}, bf16[1,6,1,32,384]{4,3,2,1,0:T(8,128)(2,1)S(1)}, u32[]{:S(2)}, u32[]{:S(2)}) collective-permute-start(bf16[1,6,1,32,384]{4,3,2,1,0:T(8,128)(2,1)S(1)} %constant_dynamic-update-slice_fusion.2), channel_id=1, source_target_pairs={{0,1},{2,3},{4,5},{6,7},{8,9},{10,11},{12,13},{14,15},{16,17},{18,... | collective-permute-start | bytes 442376 | tf_op jit(solution)/shard_map/ppermute | solution.py:21
  23.4 0.6 gather_fusion
  24.1 0.8 fusion.97
  25.0 1.3 collective-permute-start.1
  26.3 5.2 %collective-permute-start = (bf16[1,8,1,64,192]{4,3,2,1,0:T(8,128)(2,1)}, bf16[1,8,1,64,192]{4,3,2,1,0:T(8,128)(2,1)S(1)}, u32[]{:S(2)}, u32[]{:S(2)}) collective-permute-start(bf16[1,8,1,64,192]{4,3,2,1,0:T(8,128)(2,1)} %get-tuple-element.18), channel_id=1, source_target_pairs={{0,1},{2,3},{4,5},{6,7},{8,9},{10,11},{12,13},{14,15},{16,17},{18,... | collective-permute-start | bytes 589832 | tf_op jit(solution)/shard_map/ppermute | solution.py:21
  31.6 0.5 convolution_add_fusion.2
  32.1 0.5 convolution_add_fusion.1
  32.6 0.5 fusion.6
  33.4 2.3 %broadcast_in_dim.43 = bf16[8,6,32,2,384]{4,3,2,1,0:T(2,128)(2,1)S(1)} broadcast(bf16[8,6,32,384]{3,2,1,0:T(8,128)(2,1)S(1)} %bitcast.284), dimensions={0,1,2,4} | broadcast | bytes 3538944 | tf_op jit(solution)/shard_map/broadcast_in_dim | solution.py:59
  35.7 2.4 %broadcast_in_dim.44 = bf16[1,8,6,64,384]{4,3,2,1,0:T(8,128)(2,1)} reshape(bf16[8,6,32,2,384]{4,3,2,1,0:T(2,128)(2,1)S(1)} %broadcast_in_dim.43) | data formatting | bytes 4718592 | tf_op jit(solution)/shard_map/broadcast_in_dim | solution.py:59
  38.1 1.6 slice.197
  40.1 1.2 copy-done
  44.8 2.9 %copy.36 = f32[9,384,192]{2,1,0:T(8,128)} copy(f32[9,384,192]{1,2,0:T(8,128)S(1)} %fusion.9) | data formatting | bytes 5308416 | tf_op jit(solution)/shard_map/stack | solution.py:75
  47.7 5.0 %reshape.249 = f32[663552]{0:T(1024)} reshape(f32[9,384,192]{2,1,0:T(8,128)} %copy.36) | data formatting | bytes 5308416 | tf_op jit(solution)/shard_map/reshape | solution.py:75
  53.0 1.1 copy-done.3
  54.5 1.5 fusion.8
  58.7 1.4 fusion.50
  60.0 0.7 add_reduce_fusion
  61.3 1.0 reduce_sum.18
  62.7 1.3 collective-permute-start.2
  64.3 2.5 %collective-permute-done.2 = bf16[1,2,1,32,768]{4,3,1,2,0:T(8,128)(2,1)S(1)} collective-permute-done((bf16[1,2,1,32,768]{4,3,1,2,0:T(8,128)(2,1)S(1)}, bf16[1,2,1,32,768]{4,3,1,2,0:T(8,128)(2,1)S(1)}, u32[]{:S(2)}, u32[]{:S(2)}) %collective-permute-start.2) | collective-permute-done | bytes 98336 | tf_op jit(solution)/shard_map/ppermute | solution.py:11
  66.9 54.9 %all-reduce.8.cloned.1.call-done = f32[663552]{0:T(1024)} async-done(((f32[663552]{0:T(1024)}), f32[663552]{0:T(1024)}) %all-reduce.8.cloned.1.call-update) | async-done | bytes 2654224
  121.7 1.7 %dynamic-slice.1 = f32[82944]{0:T(1024)} dynamic-slice(f32[663552]{0:T(1024)} %all-reduce.8.cloned.1.call-done, u32[]{:T(128)S(6)} %multiply.1), dynamic_slice_sizes={82944} | dynamic-slice | bytes 663556
  123.8 1.0 fusion.20
  124.7 35.7 %all-reduce.6.cloned.1.call-done = f32[82944]{0:T(1024)} async-done(((f32[82944]{0:T(1024)}), f32[82944]{0:T(1024)}) %all-reduce.6.cloned.1.call-update) | async-done | bytes 331792 | tf_op jit(solution)/shard_map/psum | solution.py:86
  160.4 1.7 %broadcast_multiply_fusion = f32[82944]{0:T(1024)} fusion(f32[82944]{0:T(1024)} %all-reduce.6.cloned.1.call-done), kind=kLoop, calls=%fused_computation.107 | loop fusion | flops 82944 | bytes 663552 | tf_op jit(solution)/shard_map/mul | solution.py:87
  (65 shorter events, 9.2 us)
Async XLA Ops:
  7.2 9.0 %copy-start.7 = (u32[32]{0:T(128)S(1)}, u32[32]{0:T(128)}, u32[]{:S(2)}) copy-start(u32[32]{0:T(128)} %constant.43) | copy-start | bytes 388
  7.2 6.2 %copy-start.4 = (bf16[1,4,1,32,384]{4,3,2,1,0:T(8,128)(2,1)S(1)}, bf16[1,4,1,32,384]{4,3,2,1,0:T(8,128)(2,1)}, u32[]{:S(2)}) copy-start(bf16[1,4,1,32,384]{4,3,2,1,0:T(8,128)(2,1)} %param.6) | copy-start | bytes 294916
  7.2 7.9 %copy-start.6 = (s32[1,1,8]{2,1,0:T(1,128)S(1)}, s32[1,1,8]{2,1,0:T(1,128)}, u32[]{:S(2)}) copy-start(s32[1,1,8]{2,1,0:T(1,128)} %param.11) | copy-start | bytes 100
  9.1 14.2 %all-to-all-start = ((bf16[1,4,4,64,192]{4,3,1,0,2:T(8,128)(2,1)}), bf16[1,4,4,64,192]{4,3,1,0,2:T(8,128)(2,1)S(1)}, u32[]{:S(2)}, u32[]{:S(2)}) async-start(bf16[1,4,4,64,192]{4,3,1,0,2:T(8,128)(2,1)} %copy.29), calls=%async_computation | async-start | bytes 1048576 | tf_op jit(solution)/shard_map/all_to_all | solution.py:62
  13.4 108.3 %all-reduce.8.cloned.1.call-start = ((), (), s32[]{:S(2)}) async-start(), calls=%async_computation.2 | async-start | bytes 5308416
  13.4 4.0 %collective-permute-start.3 = (bf16[1,2,1,32,384]{4,3,2,1,0:T(8,128)(2,1)S(1)}, bf16[1,2,1,32,384]{4,3,2,1,0:T(8,128)(2,1)S(1)}, u32[]{:S(2)}, u32[]{:S(2)}) collective-permute-start(bf16[1,2,1,32,384]{4,3,2,1,0:T(8,128)(2,1)S(1)} %slice.163), channel_id=1, source_target_pairs={{0,2},{2,4},{4,6},{1,3},{3,5},{5,7},{8,10},{10,12},{12,14},{9,11},... | collective-permute-start | bytes 147464 | tf_op jit(solution)/shard_map/ppermute | solution.py:11
  17.4 14.1 %collective-permute-start.5 = (bf16[1,6,1,32,384]{4,3,2,1,0:T(8,128)(2,1)S(1)}, bf16[1,6,1,32,384]{4,3,2,1,0:T(8,128)(2,1)S(1)}, u32[]{:S(2)}, u32[]{:S(2)}) collective-permute-start(bf16[1,6,1,32,384]{4,3,2,1,0:T(8,128)(2,1)S(1)} %constant_dynamic-update-slice_fusion.2), channel_id=1, source_target_pairs={{1,0},{3,2},{5,4},{7,6},{9,8},{11,10},{13,12},{15,14},{17,16},{19,... | collective-permute-start | bytes 442376 | tf_op jit(solution)/shard_map/ppermute | solution.py:22
  18.7 12.8 %collective-permute-start.4 = (bf16[1,6,1,32,384]{4,3,2,1,0:T(8,128)(2,1)S(1)}, bf16[1,6,1,32,384]{4,3,2,1,0:T(8,128)(2,1)S(1)}, u32[]{:S(2)}, u32[]{:S(2)}) collective-permute-start(bf16[1,6,1,32,384]{4,3,2,1,0:T(8,128)(2,1)S(1)} %constant_dynamic-update-slice_fusion.2), channel_id=1, source_target_pairs={{0,1},{2,3},{4,5},{6,7},{8,9},{10,11},{12,13},{14,15},{16,17},{18,... | collective-permute-start | bytes 442376 | tf_op jit(solution)/shard_map/ppermute | solution.py:21
  24.0 7.6 %copy-start.1 = (bf16[3,384,768]{2,1,0:T(8,128)(2,1)S(1)}, bf16[3,384,768]{2,1,0:T(8,128)(2,1)}, u32[]{:S(2)}) copy-start(bf16[3,384,768]{2,1,0:T(8,128)(2,1)} %param.7) | copy-start | bytes 5308420
  24.0 7.6 %copy-start.5 = (f32[768]{0:T(1024)S(1)}, f32[768]{0:T(1024)}, u32[]{:S(2)}) copy-start(f32[768]{0:T(1024)} %param.8) | copy-start | bytes 9220
  25.0 29.5 %collective-permute-start.1 = (bf16[1,8,1,64,192]{4,3,2,1,0:T(8,128)(2,1)}, bf16[1,8,1,64,192]{4,3,2,1,0:T(8,128)(2,1)}, u32[]{:S(2)}, u32[]{:S(2)}) collective-permute-start(bf16[1,8,1,64,192]{4,3,2,1,0:T(8,128)(2,1)} %get-tuple-element.19), channel_id=1, source_target_pairs={{1,0},{3,2},{5,4},{7,6},{9,8},{11,10},{13,12},{15,14},{17,16},{19,... | collective-permute-start | bytes 589832 | tf_op jit(solution)/shard_map/ppermute | solution.py:22
  26.3 28.3 %collective-permute-start = (bf16[1,8,1,64,192]{4,3,2,1,0:T(8,128)(2,1)}, bf16[1,8,1,64,192]{4,3,2,1,0:T(8,128)(2,1)S(1)}, u32[]{:S(2)}, u32[]{:S(2)}) collective-permute-start(bf16[1,8,1,64,192]{4,3,2,1,0:T(8,128)(2,1)} %get-tuple-element.18), channel_id=1, source_target_pairs={{0,1},{2,3},{4,5},{6,7},{8,9},{10,11},{12,13},{14,15},{16,17},{18,... | collective-permute-start | bytes 589832 | tf_op jit(solution)/shard_map/ppermute | solution.py:21
  39.7 1.7 copy-start
  52.8 1.3 copy-start.3
  52.8 107.6 %all-reduce.6.cloned.1.call-start = ((), (), s32[]{:S(2)}) async-start(), calls=%async_computation.1 | async-start | bytes 663552 | tf_op jit(solution)/shard_map/psum | solution.py:86
  61.3 2.7 %copy-start.2 = (bf16[3,384,768]{2,1,0:T(8,128)(2,1)S(1)}, bf16[3,384,768]{2,1,0:T(8,128)(2,1)}, u32[]{:S(2)}) copy-start(bf16[3,384,768]{2,1,0:T(8,128)(2,1)} %param.7) | copy-start | bytes 5308420
  62.7 4.2 %collective-permute-start.2 = (bf16[1,2,1,32,768]{4,3,1,2,0:T(8,128)(2,1)S(1)}, bf16[1,2,1,32,768]{4,3,1,2,0:T(8,128)(2,1)S(1)}, u32[]{:S(2)}, u32[]{:S(2)}) collective-permute-start(bf16[1,2,1,32,768]{4,3,1,2,0:T(8,128)(2,1)S(1)} %slice.189), channel_id=1, source_target_pairs={{2,0},{4,2},{6,4},{3,1},{5,3},{7,5},{10,8},{12,10},{14,12},{11,9},... | collective-permute-start | bytes 294920 | tf_op jit(solution)/shard_map/ppermute | solution.py:11
Sparse Core Ops, SparseCore 0:
  52.9 68.7 all-reduce.7
  124.6 35.7 all-reduce.5
where the time goes:
time: 170 us; the launch traced here: 169 us
  waiting for transfers between devices  93.1 us (55%)
  local copies, waits for them, and re-layouts  23.4 us (14%)
  starting transfers between devices  19.8 us (12%)
  between operations  15.2 us (9%)
  matrix products  12 us (7%)
  other arithmetic  5.52 us (3%)
    unnamed x3, waiting for transfers between devices  54.9 us
    psum x1, waiting for transfers between devices, local(): summed = lax.psum(shard, 'clip')  35.7 us
    ppermute x2, starting transfers between devices, extended_2(): before = lax.ppermute(last, axis, up)  9.8 us
    unnamed x21, local copies, waits for them, and re-layouts  6.58 us
    dot_general x9, matrix products, local(): jnp.einsum('cfhwo,io->cfhwi', window, space_weight[tap_row, tap_col], pre...  5.12 us
    reshape x1, local copies, waits for them, and re-layouts, local(): weight_terms = jnp.stack(tap_terms).reshape(-1)  5.02 us
    broadcast_in_dim x2, local copies, waits for them, and re-layouts, local(): jnp.repeat(jnp.repeat(upsampled, 2, axis=2), 2, axis=3)[:, :, 1:up_rows + 3]  4.67 us
    all_to_all x1, starting transfers between devices, local(): lax.all_to_all(pixel_grads, 'row', split_axis=2, concat_axis=1, tiled=True)  4.26 us
  transfers between devices with their start and end apart: 9, of which 3 were waited for; matrix products, arithmetic and copies ran while one was open for 20% of the time, Pallas kernels for 0%

commit v1 on v0

--- a/solution.py
+++ b/solution.py
@@ -83,7 +83,9 @@
         * band_count
     )
     shard = lax.psum_scatter(weight_terms, ("frame", "row"), scatter_dimension=0, tiled=True)
-    summed = lax.psum(shard, "clip")
+    summed = shard
+    for hop in (1, 2):
+        summed = summed + lax.ppermute(summed, "clip", [(dev, dev ^ hop) for dev in range(4)])
     weight_grad = summed * (1.0 / math.sqrt(out_pixels))
     padded_grad = jnp.pad(grad_band, ((0, 0), (0, 0), (0, 0), (1, 1), (0, 0)))
     up_grad = jnp.zeros((1, 2 * frames, up_rows, up_width, channels), jnp.float32)

time: 170 us -> 157 us (0.924)
  waiting for transfers between devices: 93.1 us -> 76.6 us
  starting transfers between devices: 19.8 us -> 23.6 us
    psum x1 -> x0, waiting for transfers between devices: 35.7 us -> none  [local(): summed = lax.psum(shard, 'clip')]
    ppermute x0 -> x2, waiting for transfers between devices: none -> 16.6 us  [local(): lax.ppermute(summed, 'clip', [(dev, dev ^ hop) for dev in range(4)])]
    ppermute x0 -> x2, starting transfers between devices: none -> 4.02 us  [local(): lax.ppermute(summed, 'clip', [(dev, dev ^ hop) for dev in range(4)])]
    unnamed x3 -> x2, waiting for transfers between devices: 54.9 us -> 58 us
  transfers between devices with their start and end apart: 9 -> 10, of which waited for: 3 -> 4; matrix products, arithmetic and copies ran while one was open for 20% -> 21% of each run, Pallas kernels for 0% -> 0%
where the time goes in v1:
time: 157 us; the launch traced here: 156 us
  waiting for transfers between devices  76.6 us (49%)
  starting transfers between devices  23.6 us (15%)
  local copies, waits for them, and re-layouts  23 us (15%)
  between operations  15.2 us (10%)
  matrix products  12 us (8%)
  other arithmetic  5.58 us (4%)
    unnamed x2, waiting for transfers between devices  58 us
    ppermute x2, waiting for transfers between devices, local(): lax.ppermute(summed, 'clip', [(dev, dev ^ hop) for dev in range(4)])  16.6 us
    ppermute x2, starting transfers between devices, extended_2(): before = lax.ppermute(last, axis, up)  9.81 us
    unnamed x21, local copies, waits for them, and re-layouts  6.08 us
    dot_general x9, matrix products, local(): jnp.einsum('cfhwo,io->cfhwi', window, space_weight[tap_row, tap_col], pre...  5.12 us
    reshape x1, local copies, waits for them, and re-layouts, local(): weight_terms = jnp.stack(tap_terms).reshape(-1)  5.03 us
    broadcast_in_dim x2, local copies, waits for them, and re-layouts, local(): jnp.repeat(jnp.repeat(upsampled, 2, axis=2), 2, axis=3)[:, :, 1:up_rows + 3]  4.84 us
    all_to_all x1, starting transfers between devices, local(): lax.all_to_all(pixel_grads, 'row', split_axis=2, concat_axis=1, tiled=True)  4.26 us
  transfers between devices with their start and end apart: 10, of which 4 were waited for; matrix products, arithmetic and copies ran while one was open for 21% of the time, Pallas kernels for 0%

profile of v1, /device:TPU:0, one launch (start us, length us, event | category | flops | bytes accessed | tf_op | source)
XLA Modules:
  0.0 156.0 jit_solution(4863111104784416412)
XLA Ops:
  7.2 1.9 %copy.29 = bf16[1,4,4,64,192]{4,3,1,0,2:T(8,128)(2,1)} copy(bf16[1,4,4,64,192]{4,3,2,1,0:T(8,128)(2,1)} %param.10) | data formatting | bytes 786432 | tf_op args[4]
  9.1 4.3 %all-to-all-start = ((bf16[1,4,4,64,192]{4,3,1,0,2:T(8,128)(2,1)}), bf16[1,4,4,64,192]{4,3,1,0,2:T(8,128)(2,1)S(1)}, u32[]{:S(2)}, u32[]{:S(2)}) async-start(bf16[1,4,4,64,192]{4,3,1,0,2:T(8,128)(2,1)} %copy.29), calls=%async_computation | async-start | bytes 1048576 | tf_op jit(solution)/shard_map/all_to_all | solution.py:62
  13.4 1.7 %collective-permute-start.3 = (bf16[1,2,1,32,384]{4,3,2,1,0:T(8,128)(2,1)S(1)}, bf16[1,2,1,32,384]{4,3,2,1,0:T(8,128)(2,1)S(1)}, u32[]{:S(2)}, u32[]{:S(2)}) collective-permute-start(bf16[1,2,1,32,384]{4,3,2,1,0:T(8,128)(2,1)S(1)} %slice.163), channel_id=1, source_target_pairs={{0,2},{2,4},{4,6},{1,3},{3,5},{5,7},{8,10},{10,12},{12,14},{9,11},... | collective-permute-start | bytes 147464 | tf_op jit(solution)/shard_map/ppermute | solution.py:11
  15.1 1.0 sort.17
  16.1 0.6 dynamic-slice
  17.4 1.3 collective-permute-start.5
  18.7 4.6 %collective-permute-start.4 = (bf16[1,6,1,32,384]{4,3,2,1,0:T(8,128)(2,1)S(1)}, bf16[1,6,1,32,384]{4,3,2,1,0:T(8,128)(2,1)S(1)}, u32[]{:S(2)}, u32[]{:S(2)}) collective-permute-start(bf16[1,6,1,32,384]{4,3,2,1,0:T(8,128)(2,1)S(1)} %constant_dynamic-update-slice_fusion.2), channel_id=1, source_target_pairs={{0,1},{2,3},{4,5},{6,7},{8,9},{10,11},{12,13},{14,15},{16,17},{18,... | collective-permute-start | bytes 442376 | tf_op jit(solution)/shard_map/ppermute | solution.py:21
  24.1 0.8 fusion.97
  25.0 1.3 collective-permute-start.1
  26.3 5.2 %collective-permute-start = (bf16[1,8,1,64,192]{4,3,2,1,0:T(8,128)(2,1)}, bf16[1,8,1,64,192]{4,3,2,1,0:T(8,128)(2,1)S(1)}, u32[]{:S(2)}, u32[]{:S(2)}) collective-permute-start(bf16[1,8,1,64,192]{4,3,2,1,0:T(8,128)(2,1)} %get-tuple-element.18), channel_id=1, source_target_pairs={{0,1},{2,3},{4,5},{6,7},{8,9},{10,11},{12,13},{14,15},{16,17},{18,... | collective-permute-start | bytes 589832 | tf_op jit(solution)/shard_map/ppermute | solution.py:21
  33.4 2.3 %broadcast_in_dim.43 = bf16[8,6,32,2,384]{4,3,2,1,0:T(2,128)(2,1)S(1)} broadcast(bf16[8,6,32,384]{3,2,1,0:T(8,128)(2,1)S(1)} %bitcast.284), dimensions={0,1,2,4} | broadcast | bytes 3538944 | tf_op jit(solution)/shard_map/broadcast_in_dim | solution.py:59
  35.7 2.5 %broadcast_in_dim.44 = bf16[1,8,6,64,384]{4,3,2,1,0:T(8,128)(2,1)} reshape(bf16[8,6,32,2,384]{4,3,2,1,0:T(2,128)(2,1)S(1)} %broadcast_in_dim.43) | data formatting | bytes 4718592 | tf_op jit(solution)/shard_map/broadcast_in_dim | solution.py:59
  38.2 1.6 %slice.197 = bf16[1,8,4,64,384]{4,3,2,1,0:T(8,128)(2,1)S(1)} slice(bf16[1,8,6,64,384]{4,3,2,1,0:T(8,128)(2,1)} %broadcast_in_dim.44), slice={[0:1], [0:8], [1:5], [0:64], [0:384]} | slice | bytes 3145728 | tf_op jit(solution)/shard_map/slice | solution.py:59
  40.3 1.2 copy-done
  45.0 2.9 %copy.36 = f32[9,384,192]{2,1,0:T(8,128)} copy(f32[9,384,192]{1,2,0:T(8,128)S(1)} %fusion.9) | data formatting | bytes 5308416 | tf_op jit(solution)/shard_map/stack | solution.py:75
  47.9 5.0 %reshape.249 = f32[663552]{0:T(1024)} reshape(f32[9,384,192]{2,1,0:T(8,128)} %copy.36) | data formatting | bytes 5308416 | tf_op jit(solution)/shard_map/reshape | solution.py:75
  53.0 1.3 copy-done.3
  54.7 1.5 fusion.8
  58.0 1.4 fusion.50
  60.2 0.7 add_reduce_fusion
  61.5 1.0 reduce_sum.18
  62.8 58.0 %all-reduce.5.cloned.1.call-done = f32[663552]{0:T(1024)} async-done(((f32[663552]{0:T(1024)}), f32[663552]{0:T(1024)}) %all-reduce.5.cloned.1.call-update) | async-done | bytes 2654224
  120.8 1.0 dynamic-slice.1
  121.8 1.6 collective-permute-start.6
  123.7 1.3 collective-permute-start.2
  125.1 1.9 %collective-permute-done.2 = bf16[1,2,1,32,768]{4,3,1,2,0:T(8,128)(2,1)S(1)} collective-permute-done((bf16[1,2,1,32,768]{4,3,1,2,0:T(8,128)(2,1)S(1)}, bf16[1,2,1,32,768]{4,3,1,2,0:T(8,128)(2,1)S(1)}, u32[]{:S(2)}, u32[]{:S(2)}) %collective-permute-start.2) | collective-permute-done | bytes 98336 | tf_op jit(solution)/shard_map/ppermute | solution.py:11
  126.9 4.0 %collective-permute-done.6 = f32[82944]{0:T(1024)S(1)} collective-permute-done((f32[82944]{0:T(1024)S(1)}, f32[82944]{0:T(1024)S(1)}, u32[]{:S(2)}, u32[]{:S(2)}) %collective-permute-start.6) | collective-permute-done | bytes 331808 | tf_op jit(solution)/shard_map/ppermute | solution.py:88
  131.0 1.0 dynamic-slice_add_fusion
  132.0 2.5 %collective-permute-start.7 = (f32[82944]{0:T(1024)S(1)}, f32[82944]{0:T(1024)S(1)}, u32[]{:S(2)}, u32[]{:S(2)}) collective-permute-start(f32[82944]{0:T(1024)S(1)} %dynamic-slice_add_fusion), channel_id=1, source_target_pairs={{0,16},{8,24},{16,0},{24,8},{1,17},{9,25},{17,1},{25,9},{2,18},{10... | collective-permute-start | bytes 995336 | tf_op jit(solution)/shard_map/ppermute | solution.py:88
  134.8 1.0 fusion.20
  135.8 12.6 %collective-permute-done.7 = f32[82944]{0:T(1024)S(1)} collective-permute-done((f32[82944]{0:T(1024)S(1)}, f32[82944]{0:T(1024)S(1)}, u32[]{:S(2)}, u32[]{:S(2)}) %collective-permute-start.7) | collective-permute-done | bytes 331808 | tf_op jit(solution)/shard_map/ppermute | solution.py:88
  148.3 0.8 add_multiply_fusion
  (67 shorter events, 11.0 us)
Async XLA Ops:
  7.2 9.0 %copy-start.7 = (u32[32]{0:T(128)S(1)}, u32[32]{0:T(128)}, u32[]{:S(2)}) copy-start(u32[32]{0:T(128)} %constant.43) | copy-start | bytes 388
  7.2 6.2 %copy-start.4 = (bf16[1,4,1,32,384]{4,3,2,1,0:T(8,128)(2,1)S(1)}, bf16[1,4,1,32,384]{4,3,2,1,0:T(8,128)(2,1)}, u32[]{:S(2)}) copy-start(bf16[1,4,1,32,384]{4,3,2,1,0:T(8,128)(2,1)} %param.6) | copy-start | bytes 294916
  7.2 7.9 %copy-start.6 = (s32[1,1,8]{2,1,0:T(1,128)S(1)}, s32[1,1,8]{2,1,0:T(1,128)}, u32[]{:S(2)}) copy-start(s32[1,1,8]{2,1,0:T(1,128)} %param.11) | copy-start | bytes 100
  9.1 14.2 %all-to-all-start = ((bf16[1,4,4,64,192]{4,3,1,0,2:T(8,128)(2,1)}), bf16[1,4,4,64,192]{4,3,1,0,2:T(8,128)(2,1)S(1)}, u32[]{:S(2)}, u32[]{:S(2)}) async-start(bf16[1,4,4,64,192]{4,3,1,0,2:T(8,128)(2,1)} %copy.29), calls=%async_computation | async-start | bytes 1048576 | tf_op jit(solution)/shard_map/all_to_all | solution.py:62
  13.4 107.4 %all-reduce.5.cloned.1.call-start = ((), (), s32[]{:S(2)}) async-start(), calls=%async_computation.1 | async-start | bytes 5308416
  13.4 4.0 %collective-permute-start.3 = (bf16[1,2,1,32,384]{4,3,2,1,0:T(8,128)(2,1)S(1)}, bf16[1,2,1,32,384]{4,3,2,1,0:T(8,128)(2,1)S(1)}, u32[]{:S(2)}, u32[]{:S(2)}) collective-permute-start(bf16[1,2,1,32,384]{4,3,2,1,0:T(8,128)(2,1)S(1)} %slice.163), channel_id=1, source_target_pairs={{0,2},{2,4},{4,6},{1,3},{3,5},{5,7},{8,10},{10,12},{12,14},{9,11},... | collective-permute-start | bytes 147464 | tf_op jit(solution)/shard_map/ppermute | solution.py:11
  17.4 14.1 %collective-permute-start.5 = (bf16[1,6,1,32,384]{4,3,2,1,0:T(8,128)(2,1)S(1)}, bf16[1,6,1,32,384]{4,3,2,1,0:T(8,128)(2,1)S(1)}, u32[]{:S(2)}, u32[]{:S(2)}) collective-permute-start(bf16[1,6,1,32,384]{4,3,2,1,0:T(8,128)(2,1)S(1)} %constant_dynamic-update-slice_fusion.2), channel_id=1, source_target_pairs={{1,0},{3,2},{5,4},{7,6},{9,8},{11,10},{13,12},{15,14},{17,16},{19,... | collective-permute-start | bytes 442376 | tf_op jit(solution)/shard_map/ppermute | solution.py:22
  18.7 12.8 %collective-permute-start.4 = (bf16[1,6,1,32,384]{4,3,2,1,0:T(8,128)(2,1)S(1)}, bf16[1,6,1,32,384]{4,3,2,1,0:T(8,128)(2,1)S(1)}, u32[]{:S(2)}, u32[]{:S(2)}) collective-permute-start(bf16[1,6,1,32,384]{4,3,2,1,0:T(8,128)(2,1)S(1)} %constant_dynamic-update-slice_fusion.2), channel_id=1, source_target_pairs={{0,1},{2,3},{4,5},{6,7},{8,9},{10,11},{12,13},{14,15},{16,17},{18,... | collective-permute-start | bytes 442376 | tf_op jit(solution)/shard_map/ppermute | solution.py:21
  24.0 7.6 %copy-start.1 = (bf16[3,384,768]{2,1,0:T(8,128)(2,1)S(1)}, bf16[3,384,768]{2,1,0:T(8,128)(2,1)}, u32[]{:S(2)}) copy-start(bf16[3,384,768]{2,1,0:T(8,128)(2,1)} %param.7) | copy-start | bytes 5308420
  24.0 7.6 %copy-start.5 = (f32[768]{0:T(1024)S(1)}, f32[768]{0:T(1024)}, u32[]{:S(2)}) copy-start(f32[768]{0:T(1024)} %param.8) | copy-start | bytes 9220
  25.0 29.7 %collective-permute-start.1 = (bf16[1,8,1,64,192]{4,3,2,1,0:T(8,128)(2,1)}, bf16[1,8,1,64,192]{4,3,2,1,0:T(8,128)(2,1)}, u32[]{:S(2)}, u32[]{:S(2)}) collective-permute-start(bf16[1,8,1,64,192]{4,3,2,1,0:T(8,128)(2,1)} %get-tuple-element.19), channel_id=1, source_target_pairs={{1,0},{3,2},{5,4},{7,6},{9,8},{11,10},{13,12},{15,14},{17,16},{19,... | collective-permute-start | bytes 589832 | tf_op jit(solution)/shard_map/ppermute | solution.py:22
  26.3 28.4 %collective-permute-start = (bf16[1,8,1,64,192]{4,3,2,1,0:T(8,128)(2,1)}, bf16[1,8,1,64,192]{4,3,2,1,0:T(8,128)(2,1)S(1)}, u32[]{:S(2)}, u32[]{:S(2)}) collective-permute-start(bf16[1,8,1,64,192]{4,3,2,1,0:T(8,128)(2,1)} %get-tuple-element.18), channel_id=1, source_target_pairs={{0,1},{2,3},{4,5},{6,7},{8,9},{10,11},{12,13},{14,15},{16,17},{18,... | collective-permute-start | bytes 589832 | tf_op jit(solution)/shard_map/ppermute | solution.py:21
  39.9 1.7 %copy-start = (bf16[1,8,6,64,384]{4,3,2,1,0:T(8,128)(2,1)S(1)}, bf16[1,8,6,64,384]{4,3,2,1,0:T(8,128)(2,1)}, u32[]{:S(2)}) copy-start(bf16[1,8,6,64,384]{4,3,2,1,0:T(8,128)(2,1)} %broadcast_in_dim.44) | copy-start | bytes 7077892
  52.9 1.3 copy-start.3
  61.4 61.9 %copy-start.2 = (bf16[3,384,768]{2,1,0:T(8,128)(2,1)S(1)}, bf16[3,384,768]{2,1,0:T(8,128)(2,1)}, u32[]{:S(2)}) copy-start(bf16[3,384,768]{2,1,0:T(8,128)(2,1)} %param.7) | copy-start | bytes 5308420
  121.8 9.2 %collective-permute-start.6 = (f32[82944]{0:T(1024)S(1)}, f32[82944]{0:T(1024)S(1)}, u32[]{:S(2)}, u32[]{:S(2)}) collective-permute-start(f32[82944]{0:T(1024)S(1)} %dynamic-slice.1), channel_id=1, source_target_pairs={{0,8},{8,0},{16,24},{24,16},{1,9},{9,1},{17,25},{25,17},{2,10},{10... | collective-permute-start | bytes 995336 | tf_op jit(solution)/shard_map/ppermute | solution.py:88
  123.7 3.2 %collective-permute-start.2 = (bf16[1,2,1,32,768]{4,3,1,2,0:T(8,128)(2,1)S(1)}, bf16[1,2,1,32,768]{4,3,1,2,0:T(8,128)(2,1)S(1)}, u32[]{:S(2)}, u32[]{:S(2)}) collective-permute-start(bf16[1,2,1,32,768]{4,3,1,2,0:T(8,128)(2,1)S(1)} %slice.189), channel_id=1, source_target_pairs={{2,0},{4,2},{6,4},{3,1},{5,3},{7,5},{10,8},{12,10},{14,12},{11,9},... | collective-permute-start | bytes 294920 | tf_op jit(solution)/shard_map/ppermute | solution.py:11
  132.0 16.3 %collective-permute-start.7 = (f32[82944]{0:T(1024)S(1)}, f32[82944]{0:T(1024)S(1)}, u32[]{:S(2)}, u32[]{:S(2)}) collective-permute-start(f32[82944]{0:T(1024)S(1)} %dynamic-slice_add_fusion), channel_id=1, source_target_pairs={{0,16},{8,24},{16,0},{24,8},{1,17},{9,25},{17,1},{25,9},{2,18},{10... | collective-permute-start | bytes 995336 | tf_op jit(solution)/shard_map/ppermute | solution.py:88
Sparse Core Ops, SparseCore 0:
  53.1 67.6 all-reduce.4
